TPU v7x, 256 devices: a whole 4x4x8 slice. The times are simulated.
256 devices in a mesh: table: 16 (over y, x), blk: 16 (over z, core).
Axes of the slice: x: 4, y: 4, z: 8, core: 2. Of those that a mesh axis runs over, the one named last changes fastest.
Arguments:
- cold_table: bfloat16 [524288, 128], P('table'), may hold values from -6 to 6
- slot_row: int32 [4096, 2048], P(('table', 'blk')), may hold values from 0 to 32767
- slot_sample: int32 [4096, 2048], P(('table', 'blk')), may hold values from 0 to 511
- slot_count: int32 [4096, 2048], P(('table', 'blk')), may hold values from 0 to 15, as said below
- hot_table: bfloat16 [4096, 128], replicated, may hold values from -6 to 6
- hot_index: int32 [131072, 8], P(('table', 'blk')), may hold values from 0 to 4095
- hot_count: int32 [131072, 8], P(('table', 'blk')), may hold values from 1 to 15
- hot_cotangent: bfloat16 [131072, 128], P(('table', 'blk')), may hold values from -0.59765625 to 0.59765625
Outputs:
- features: bfloat16 [131072, 256], P(('table', 'blk'))
- hot_grad: float32 [4096, 128], P('blk')
Inputs may be any that keep to these rules, and one draw needn't show every extreme that they name: `slot_count`: slots of a bucket that carry no request have count 0 and follow its used slots; in every draw, for every index of blk, one cold shard receives 2048 used slots from every device with that index.
All inputs are finite; a program needn't handle non-finite values.
Results may differ from a plain program's by a relative error of at most 0.001.
Values may be sent and summed in bfloat16 or wider, within the bound.
No kernel may reach another device: no remote copies, remote signals or barrier semaphores. Data moves between devices by JAX's collectives and lax.ppermute only.
A program may use at most 128 MiB of HBM per device.

v0:
```python
import jax
import jax.numpy as jnp
from jax import lax
from jax.sharding import PartitionSpec as P

cold_scale = 0.03125
hot_scale = 0.0625


def incidence_pool(sample_idx, counts, picked, samples):
    matches = jnp.arange(samples, dtype=jnp.int32)[:, None] == sample_idx[None, :]
    weights = jnp.where(matches, counts[None, :].astype(jnp.float32) * cold_scale, 0.0).astype(
        jnp.bfloat16
    )
    return jnp.dot(weights, picked, preferred_element_type=jnp.float32)


def hot_incidence(hot_index, hot_count, hot_rows):
    row_ids = jnp.arange(hot_rows, dtype=jnp.int32)[None, :]
    hot_weights = hot_count.astype(jnp.float32) * hot_scale
    lookups = hot_index.shape[1]

    def add_lookup(step, total):
        index_col = lax.dynamic_slice_in_dim(hot_index, step, 1, 1)
        weight_col = lax.dynamic_slice_in_dim(hot_weights, step, 1, 1)
        return total + jnp.where(index_col == row_ids, weight_col, 0.0)

    empty = jnp.zeros((hot_index.shape[0], hot_rows), jnp.float32)
    return lax.fori_loop(0, lookups, add_lookup, empty).astype(jnp.bfloat16)


def shards(
    cold_table, slot_row, slot_sample, slot_count, hot_table, hot_index, hot_count, hot_cotangent
):
    samples = hot_index.shape[0]
    width = cold_table.shape[1]
    got_row = lax.all_to_all(slot_row, "table", split_axis=0, concat_axis=0, tiled=True)
    picked = jnp.take(cold_table, got_row, axis=0)
    returned = lax.all_to_all(picked, "table", split_axis=0, concat_axis=0, tiled=True)

    def add_owner(total, packed):
        return (total + incidence_pool(packed[0], packed[1], packed[2], samples), None)

    cold_pooled, _ = lax.scan(
        add_owner, jnp.zeros((samples, width), jnp.float32), (slot_sample, slot_count, returned)
    )
    hot_rows = hot_table.shape[0]
    incidence = hot_incidence(hot_index, hot_count, hot_rows)
    hot_pooled = jnp.dot(incidence, hot_table, preferred_element_type=jnp.float32)
    features = jnp.concatenate(
        [cold_pooled.astype(jnp.bfloat16), hot_pooled.astype(jnp.bfloat16)], axis=1
    )
    local_sums = lax.dot_general(
        incidence, hot_cotangent, (((0,), (0,)), ((), ())), preferred_element_type=jnp.float32
    )
    share_rows = lax.psum_scatter(local_sums, "blk", scatter_dimension=0, tiled=True)
    hot_grad = lax.psum(share_rows, "table")
    return (features, hot_grad)


def solution(mesh):
    return jax.shard_map(
        shards,
        mesh=mesh,
        in_specs=(
            P("table", None),
            P(("table", "blk"), None),
            P(("table", "blk"), None),
            P(("table", "blk"), None),
            P(),
            P(("table", "blk"), None),
            P(("table", "blk"), None),
            P(("table", "blk"), None),
        ),
        out_specs=(P(("table", "blk"), None), P("blk", None)),
        check_vma=False,
    )
```

profile of v0, /device:TPU:2, one launch (start us, length us, event | category | flops | bytes accessed | tf_op | source)
XLA Modules:
  0.0 381.2 jit_solution(16679746886880917182)
XLA Ops:
  8.9 7.5 %all-to-all-start = ((s32[16,1,2048]{2,1,0:T(1,128)}), s32[16,1,2048]{2,1,0:T(1,128)S(1)}, u32[]{:S(2)}, u32[]{:S(2)}) async-start(s32[16,1,2048]{2,1,0:T(1,128)} %all_to_all.13), calls=%async_computation | async-start | bytes 262144 | tf_op jit(solution)/shard_map/all_to_all | solution.py:37
  17.1 5.9 %all-to-all-done = s32[16,1,2048]{2,1,0:T(1,128)S(1)} async-done(((s32[16,1,2048]{2,1,0:T(1,128)}), s32[16,1,2048]{2,1,0:T(1,128)S(1)}, u32[]{:S(2)}, u32[]{:S(2)}) %all-to-all-start) | async-done | bytes 131104 | tf_op jit(solution)/shard_map/all_to_all | solution.py:37
  23.2 114.6 %gather_fusion = bf16[32768,128]{1,0:T(8,128)(2,1)} fusion(bf16[32768,128]{1,0:T(8,128)(2,1)} %param.12, s32[32768]{0:T(1024)S(1)} %broadcast_clamp_fusion), kind=kCustom, calls=%fused_computation | custom fusion | bytes 16908288 | tf_op jit(solution)/shard_map/jit(_take)/gather | solution.py:38
  137.9 7.9 %broadcast_select_fusion = bf16[16,2048,128]{2,1,0:T(8,128)(2,1)} fusion(bf16[16,2048,128]{2,1,0:T(8,128)(2,1)} %bitcast.27, pred[16,2048]{1,0:T(8,128)(4,1)S(1)} %compare_and_fusion), kind=kLoop, calls=%fused_computation.19 | loop fusion | flops 4194304 | bytes 16809984 | tf_op jit(solution)/shard_map/jit(_take)/select_n | solution.py:38
  145.8 6.0 %all-to-all-start.1 = ((bf16[16,2048,128]{2,1,0:T(8,128)(2,1)}), bf16[16,2048,128]{2,1,0:T(8,128)(2,1)}, u32[]{:S(2)}, u32[]{:S(2)}) async-start(bf16[16,2048,128]{2,1,0:T(8,128)(2,1)} %broadcast_select_fusion), calls=%async_computation.1 | async-start | bytes 16777216 | tf_op jit(solution)/shard_map/all_to_all | solution.py:39
  151.8 56.0 %while.26 = (s32[]{:T(128)}, f32[512,4096]{1,0:T(8,128)}, s32[512,8]{0,1:T(8,128)}, f32[512,8]{0,1:T(8,128)S(1)}, s32[]{:T(128)}, /*index=5*/s32[]{:T(128)}) while((s32[]{:T(128)}, f32[512,4096]{1,0:T(8,128)}, s32[512,8]{0,1:T(8,128)}, f32[512,8]{0,1:T(8,128)S(1)}, s32[]{:T(128)}, /*index=5*/s32[]{:T(128)}) %tuple.55), condition=%wide.region_3.4_spmd.clone, body=%wide.region_2.3_spmd.clone.sunk | while | flops 8388611 | bytes 16789588 | solution.py:29
  152.6 4.4 %select_add_fusion.2 = f32[512,4096]{1,0:T(8,128)} fusion(f32[512,4096]{1,0:T(8,128)} %get-tuple-element.245, f32[512]{0:T(512)S(1)} %bitcast.29, s32[512]{0:T(512)S(1)} %bitcast.30, pred[]{:T(512)S(6)} %compare.7), kind=kLoop, calls=%fused_computation.16.clone.1 | loop fusion | flops 8388608 | bytes 16781312 | tf_op jit(solution)/shard_map/while/body/eval_jaxpr/add | solution.py:26
  157.6 6.5 %select_add_fusion.2 = f32[512,4096]{1,0:T(8,128)} fusion(f32[512,4096]{1,0:T(8,128)} %get-tuple-element.245, f32[512]{0:T(512)S(1)} %bitcast.29, s32[512]{0:T(512)S(1)} %bitcast.30, pred[]{:T(512)S(6)} %compare.7), kind=kLoop, calls=%fused_computation.16.clone.1 | loop fusion | flops 8388608 | bytes 16781312 | tf_op jit(solution)/shard_map/while/body/eval_jaxpr/add | solution.py:26
  164.9 6.5 %select_add_fusion.2 = f32[512,4096]{1,0:T(8,128)} fusion(f32[512,4096]{1,0:T(8,128)} %get-tuple-element.245, f32[512]{0:T(512)S(1)} %bitcast.29, s32[512]{0:T(512)S(1)} %bitcast.30, pred[]{:T(512)S(6)} %compare.7), kind=kLoop, calls=%fused_computation.16.clone.1 | loop fusion | flops 8388608 | bytes 16781312 | tf_op jit(solution)/shard_map/while/body/eval_jaxpr/add | solution.py:26
  172.2 6.5 %select_add_fusion.2 = f32[512,4096]{1,0:T(8,128)} fusion(f32[512,4096]{1,0:T(8,128)} %get-tuple-element.245, f32[512]{0:T(512)S(1)} %bitcast.29, s32[512]{0:T(512)S(1)} %bitcast.30, pred[]{:T(512)S(6)} %compare.7), kind=kLoop, calls=%fused_computation.16.clone.1 | loop fusion | flops 8388608 | bytes 16781312 | tf_op jit(solution)/shard_map/while/body/eval_jaxpr/add | solution.py:26
  179.4 6.5 %select_add_fusion.2 = f32[512,4096]{1,0:T(8,128)} fusion(f32[512,4096]{1,0:T(8,128)} %get-tuple-element.245, f32[512]{0:T(512)S(1)} %bitcast.29, s32[512]{0:T(512)S(1)} %bitcast.30, pred[]{:T(512)S(6)} %compare.7), kind=kLoop, calls=%fused_computation.16.clone.1 | loop fusion | flops 8388608 | bytes 16781312 | tf_op jit(solution)/shard_map/while/body/eval_jaxpr/add | solution.py:26
  186.7 6.5 %select_add_fusion.2 = f32[512,4096]{1,0:T(8,128)} fusion(f32[512,4096]{1,0:T(8,128)} %get-tuple-element.245, f32[512]{0:T(512)S(1)} %bitcast.29, s32[512]{0:T(512)S(1)} %bitcast.30, pred[]{:T(512)S(6)} %compare.7), kind=kLoop, calls=%fused_computation.16.clone.1 | loop fusion | flops 8388608 | bytes 16781312 | tf_op jit(solution)/shard_map/while/body/eval_jaxpr/add | solution.py:26
  194.0 6.5 %select_add_fusion.2 = f32[512,4096]{1,0:T(8,128)} fusion(f32[512,4096]{1,0:T(8,128)} %get-tuple-element.245, f32[512]{0:T(512)S(1)} %bitcast.29, s32[512]{0:T(512)S(1)} %bitcast.30, pred[]{:T(512)S(6)} %compare.7), kind=kLoop, calls=%fused_computation.16.clone.1 | loop fusion | flops 8388608 | bytes 16781312 | tf_op jit(solution)/shard_map/while/body/eval_jaxpr/add | solution.py:26
  201.2 6.5 %select_add_fusion.2 = f32[512,4096]{1,0:T(8,128)} fusion(f32[512,4096]{1,0:T(8,128)} %get-tuple-element.245, f32[512]{0:T(512)S(1)} %bitcast.29, s32[512]{0:T(512)S(1)} %bitcast.30, pred[]{:T(512)S(6)} %compare.7), kind=kLoop, calls=%fused_computation.16.clone.1 | loop fusion | flops 8388608 | bytes 16781312 | tf_op jit(solution)/shard_map/while/body/eval_jaxpr/add | solution.py:26
  207.7 6.0 %fusion.11 = f32[4096,128]{1,0:T(8,128)} fusion(bf16[512,128]{1,0:T(8,128)(2,1)S(1)} %copy-done.1, f32[512,4096]{1,0:T(8,128)} %get-tuple-element.124), kind=kOutput, calls=%fused_computation.20 | convolution fusion | flops 538968064 | bytes 10616832 | tf_op jit(solution)/shard_map/dot_general | solution.py:53
  213.9 4.9 %fusion.15 = bf16[512,128]{0,1:T(8,128)(2,1)S(1)} fusion(bf16[4096,128]{1,0:T(8,128)(2,1)S(1)} %copy-done, f32[512,4096]{1,0:T(8,128)} %get-tuple-element.124), kind=kOutput, calls=%fused_computation.24 | convolution fusion | flops 539033600 | bytes 9568256 | tf_op jit(solution)/shard_map/dot_general | solution.py:49
  218.8 58.8 %reduce-scatter.2.cloned.1.call-done = f32[256,128]{1,0:T(8,128)} async-done(((f32[4096,128]{1,0:T(8,128)}), f32[256,128]{1,0:T(8,128)}) %reduce-scatter.2.cloned.1.call-update) | async-done | bytes 131088 | tf_op jit(solution)/shard_map/reduce_scatter | solution.py:56
  277.6 56.7 %while.25 = (s32[]{:T(128)}, f32[512,128]{1,0:T(8,128)S(1)}, s32[16,2048]{1,0:T(8,128)}, s32[16,2048]{1,0:T(8,128)}, bf16[16,2048,128]{2,1,0:T(8,128)(2,1)}, /*index=5*/s32[]{:T(128)}, s32[]{:T(128)}) while((s32[]{:T(128)}, f32[512,128]{1,0:T(8,128)S(1)}, s32[16,2048]{1,0:T(8,128)}, s32[16,2048]{1,0:T(8,128)}, ...), condition=%wide.region_1.2_spmd.clone, body=%wide.region_0.1_spmd.clone.sunk | while | flops 270667776 | bytes 1098335 | solution.py:44
  279.4 1.8 fusion.23
  286.4 1.8 fusion.23
  290.0 1.8 fusion.23
  325.4 1.8 fusion.23
  332.5 1.8 fusion.23
  335.3 37.5 %all-reduce.2.cloned.1.call-done = f32[256,128]{1,0:T(8,128)} async-done(((f32[256,128]{1,0:T(8,128)}), f32[256,128]{1,0:T(8,128)}) %all-reduce.2.cloned.1.call-update) | async-done | bytes 131088 | tf_op jit(solution)/shard_map/psum | solution.py:57
  (79 shorter events, 58.4 us)
Async XLA Ops:
  7.2 206.7 %copy-start = (bf16[4096,128]{1,0:T(8,128)(2,1)S(1)}, bf16[4096,128]{1,0:T(8,128)(2,1)}, u32[]{:S(2)}) copy-start(bf16[4096,128]{1,0:T(8,128)(2,1)} %param.16) | copy-start | bytes 3145732
  8.9 14.1 %all-to-all-start = ((s32[16,1,2048]{2,1,0:T(1,128)}), s32[16,1,2048]{2,1,0:T(1,128)S(1)}, u32[]{:S(2)}, u32[]{:S(2)}) async-start(s32[16,1,2048]{2,1,0:T(1,128)} %all_to_all.13), calls=%async_computation | async-start | bytes 262144 | tf_op jit(solution)/shard_map/all_to_all | solution.py:37
  145.8 131.9 %all-to-all-start.1 = ((bf16[16,2048,128]{2,1,0:T(8,128)(2,1)}), bf16[16,2048,128]{2,1,0:T(8,128)(2,1)}, u32[]{:S(2)}, u32[]{:S(2)}) async-start(bf16[16,2048,128]{2,1,0:T(8,128)(2,1)} %broadcast_select_fusion), calls=%async_computation.1 | async-start | bytes 16777216 | tf_op jit(solution)/shard_map/all_to_all | solution.py:39
  151.7 125.9 %reduce-scatter.2.cloned.1.call-start = ((), (), s32[]{:S(2)}) async-start(), calls=%async_computation.3 | async-start | bytes 2228224 | tf_op jit(solution)/shard_map/reduce_scatter | solution.py:56
  151.8 56.0 %copy-start.1 = (bf16[512,128]{1,0:T(8,128)(2,1)S(1)}, bf16[512,128]{1,0:T(8,128)(2,1)}, u32[]{:S(2)}) copy-start(bf16[512,128]{1,0:T(8,128)(2,1)} %param.19) | copy-start | bytes 393220
  213.8 159.0 %all-reduce.2.cloned.1.call-start = ((), (), s32[]{:S(2)}) async-start(), calls=%async_computation.4 | async-start | bytes 262144 | tf_op jit(solution)/shard_map/psum | solution.py:57
Sparse Core Ops, SparseCore 0:
  213.9 63.6 reduce-scatter.1
  280.8 92.0 all-reduce.1
where the time goes:
time: 384 us; the launch traced here: 381 us
  local copies, waits for them, and re-layouts  138 us (36%)
  waiting for transfers between devices  102 us (27%)
  other arithmetic  72.6 us (19%)
  matrix products  39.8 us (10%)
  between operations  14.1 us (4%)
  starting transfers between devices  13.5 us (4%)
    gather x1, local copies, waits for them, and re-layouts, shards(): picked = jnp.take(cold_table, got_row, axis=0)  115 us
    reduce_scatter x1, waiting for transfers between devices, shards(): lax.psum_scatter(local_sums, 'blk', scatter_dimension=0, tiled=True)  58.8 us
    add x8, other arithmetic, add_lookup(): return total + jnp.where(index_col == row_ids, weight_col, 0.0)  50.1 us
    psum x1, waiting for transfers between devices, shards(): hot_grad = lax.psum(share_rows, 'table')  37.5 us
    dot_general x16, matrix products, incidence_pool(): return jnp.dot(weights, picked, preferred_element_type=jnp.float32)  28.9 us
    mul x16, other arithmetic, incidence_pool(): counts[None, :].astype(jnp.float32) * cold_scale  13.7 us
    dynamic_slice x16, local copies, waits for them, and re-layouts, shards(): lax.scan(add_owner, jnp.zeros((samples, width), jnp.float32), (slot_sampl...  13.7 us
    select_n x2, other arithmetic, shards(): picked = jnp.take(cold_table, got_row, axis=0)  8.02 us
  transfers between devices with their start and end apart: 4, of which 3 were waited for; matrix products, arithmetic and copies ran while one was open for 33% of the time, Pallas kernels for 0%

commit v1 on v0

--- a/solution.py
+++ b/solution.py
@@ -54,7 +54,7 @@
         incidence, hot_cotangent, (((0,), (0,)), ((), ())), preferred_element_type=jnp.float32
     )
     share_rows = lax.psum_scatter(local_sums, "blk", scatter_dimension=0, tiled=True)
-    hot_grad = lax.psum(share_rows, "table")
+    hot_grad = jnp.sum(lax.all_gather(share_rows, "table"), axis=0)
     return (features, hot_grad)
 
 

time: 384 us -> 349 us (0.909)
  waiting for transfers between devices: 102 us -> 64.8 us
    psum x1 -> x0, waiting for transfers between devices: 37.5 us -> none  [shards(): hot_grad = lax.psum(share_rows, 'table')]
  transfers between devices with their start and end apart: 4 -> 4, of which waited for: 3 -> 2; matrix products, arithmetic and copies ran while one was open for 33% -> 36% of each run, Pallas kernels for 0% -> 0%
where the time goes in v1:
time: 349 us; the launch traced here: 345 us
  local copies, waits for them, and re-layouts  137 us (39%)
  other arithmetic  75 us (21%)
  waiting for transfers between devices  64.8 us (19%)
  matrix products  39.8 us (11%)
  between operations  14.1 us (4%)
  starting transfers between devices  13.5 us (4%)
    gather x1, local copies, waits for them, and re-layouts, shards(): picked = jnp.take(cold_table, got_row, axis=0)  115 us
    reduce_scatter x1, waiting for transfers between devices, shards(): lax.psum_scatter(local_sums, 'blk', scatter_dimension=0, tiled=True)  58.8 us
    add x8, other arithmetic, add_lookup(): return total + jnp.where(index_col == row_ids, weight_col, 0.0)  50.1 us
    dot_general x16, matrix products, incidence_pool(): return jnp.dot(weights, picked, preferred_element_type=jnp.float32)  28.9 us
    mul x16, other arithmetic, incidence_pool(): counts[None, :].astype(jnp.float32) * cold_scale  13.7 us
    dynamic_slice x16, local copies, waits for them, and re-layouts, shards(): lax.scan(add_owner, jnp.zeros((samples, width), jnp.float32), (slot_sampl...  13.7 us
    select_n x2, other arithmetic, shards(): picked = jnp.take(cold_table, got_row, axis=0)  8.02 us
    all_to_all x1, starting transfers between devices, shards(): lax.all_to_all(slot_row, 'table', split_axis=0, concat_axis=0, tiled=True)  7.48 us
  transfers between devices with their start and end apart: 4, of which 2 were waited for; matrix products, arithmetic and copies ran while one was open for 36% of the time, Pallas kernels for 0%

profile of v1, /device:TPU:2, one launch (start us, length us, event | category | flops | bytes accessed | tf_op | source)
XLA Modules:
  0.0 344.5 jit_solution(14211295256408409577)
XLA Ops:
  8.9 7.5 %all-to-all-start = ((s32[16,1,2048]{2,1,0:T(1,128)}), s32[16,1,2048]{2,1,0:T(1,128)S(1)}, u32[]{:S(2)}, u32[]{:S(2)}) async-start(s32[16,1,2048]{2,1,0:T(1,128)} %all_to_all.13), calls=%async_computation | async-start | bytes 262144 | tf_op jit(solution)/shard_map/all_to_all | solution.py:37
  17.1 5.9 %all-to-all-done = s32[16,1,2048]{2,1,0:T(1,128)S(1)} async-done(((s32[16,1,2048]{2,1,0:T(1,128)}), s32[16,1,2048]{2,1,0:T(1,128)S(1)}, u32[]{:S(2)}, u32[]{:S(2)}) %all-to-all-start) | async-done | bytes 131104 | tf_op jit(solution)/shard_map/all_to_all | solution.py:37
  23.2 114.6 %gather_fusion = bf16[32768,128]{1,0:T(8,128)(2,1)} fusion(bf16[32768,128]{1,0:T(8,128)(2,1)} %param.12, s32[32768]{0:T(1024)S(1)} %broadcast_clamp_fusion), kind=kCustom, calls=%fused_computation | custom fusion | bytes 16908288 | tf_op jit(solution)/shard_map/jit(_take)/gather | solution.py:38
  137.9 7.9 %broadcast_select_fusion = bf16[16,2048,128]{2,1,0:T(8,128)(2,1)} fusion(bf16[16,2048,128]{2,1,0:T(8,128)(2,1)} %bitcast.28, pred[16,2048]{1,0:T(8,128)(4,1)S(1)} %compare_and_fusion), kind=kLoop, calls=%fused_computation.19 | loop fusion | flops 4194304 | bytes 16809984 | tf_op jit(solution)/shard_map/jit(_take)/select_n | solution.py:38
  145.8 6.0 %all-to-all-start.1 = ((bf16[16,2048,128]{2,1,0:T(8,128)(2,1)}), bf16[16,2048,128]{2,1,0:T(8,128)(2,1)}, u32[]{:S(2)}, u32[]{:S(2)}) async-start(bf16[16,2048,128]{2,1,0:T(8,128)(2,1)} %broadcast_select_fusion), calls=%async_computation.1 | async-start | bytes 16777216 | tf_op jit(solution)/shard_map/all_to_all | solution.py:39
  151.8 56.0 %while.26 = (s32[]{:T(128)}, f32[512,4096]{1,0:T(8,128)}, s32[512,8]{0,1:T(8,128)}, f32[512,8]{0,1:T(8,128)S(1)}, s32[]{:T(128)}, /*index=5*/s32[]{:T(128)}) while((s32[]{:T(128)}, f32[512,4096]{1,0:T(8,128)}, s32[512,8]{0,1:T(8,128)}, f32[512,8]{0,1:T(8,128)S(1)}, s32[]{:T(128)}, /*index=5*/s32[]{:T(128)}) %tuple.55), condition=%wide.region_3.4_spmd.clone, body=%wide.region_2.3_spmd.clone.sunk | while | flops 8388611 | bytes 16789588 | solution.py:29
  152.6 4.4 %select_add_fusion.2 = f32[512,4096]{1,0:T(8,128)} fusion(f32[512,4096]{1,0:T(8,128)} %get-tuple-element.245, f32[512]{0:T(512)S(1)} %bitcast.31, s32[512]{0:T(512)S(1)} %bitcast.32, pred[]{:T(512)S(6)} %compare.7), kind=kLoop, calls=%fused_computation.16.clone.1 | loop fusion | flops 8388608 | bytes 16781312 | tf_op jit(solution)/shard_map/while/body/eval_jaxpr/add | solution.py:26
  157.6 6.5 %select_add_fusion.2 = f32[512,4096]{1,0:T(8,128)} fusion(f32[512,4096]{1,0:T(8,128)} %get-tuple-element.245, f32[512]{0:T(512)S(1)} %bitcast.31, s32[512]{0:T(512)S(1)} %bitcast.32, pred[]{:T(512)S(6)} %compare.7), kind=kLoop, calls=%fused_computation.16.clone.1 | loop fusion | flops 8388608 | bytes 16781312 | tf_op jit(solution)/shard_map/while/body/eval_jaxpr/add | solution.py:26
  164.9 6.5 %select_add_fusion.2 = f32[512,4096]{1,0:T(8,128)} fusion(f32[512,4096]{1,0:T(8,128)} %get-tuple-element.245, f32[512]{0:T(512)S(1)} %bitcast.31, s32[512]{0:T(512)S(1)} %bitcast.32, pred[]{:T(512)S(6)} %compare.7), kind=kLoop, calls=%fused_computation.16.clone.1 | loop fusion | flops 8388608 | bytes 16781312 | tf_op jit(solution)/shard_map/while/body/eval_jaxpr/add | solution.py:26
  172.2 6.5 %select_add_fusion.2 = f32[512,4096]{1,0:T(8,128)} fusion(f32[512,4096]{1,0:T(8,128)} %get-tuple-element.245, f32[512]{0:T(512)S(1)} %bitcast.31, s32[512]{0:T(512)S(1)} %bitcast.32, pred[]{:T(512)S(6)} %compare.7), kind=kLoop, calls=%fused_computation.16.clone.1 | loop fusion | flops 8388608 | bytes 16781312 | tf_op jit(solution)/shard_map/while/body/eval_jaxpr/add | solution.py:26
  179.4 6.5 %select_add_fusion.2 = f32[512,4096]{1,0:T(8,128)} fusion(f32[512,4096]{1,0:T(8,128)} %get-tuple-element.245, f32[512]{0:T(512)S(1)} %bitcast.31, s32[512]{0:T(512)S(1)} %bitcast.32, pred[]{:T(512)S(6)} %compare.7), kind=kLoop, calls=%fused_computation.16.clone.1 | loop fusion | flops 8388608 | bytes 16781312 | tf_op jit(solution)/shard_map/while/body/eval_jaxpr/add | solution.py:26
  186.7 6.5 %select_add_fusion.2 = f32[512,4096]{1,0:T(8,128)} fusion(f32[512,4096]{1,0:T(8,128)} %get-tuple-element.245, f32[512]{0:T(512)S(1)} %bitcast.31, s32[512]{0:T(512)S(1)} %bitcast.32, pred[]{:T(512)S(6)} %compare.7), kind=kLoop, calls=%fused_computation.16.clone.1 | loop fusion | flops 8388608 | bytes 16781312 | tf_op jit(solution)/shard_map/while/body/eval_jaxpr/add | solution.py:26
  194.0 6.5 %select_add_fusion.2 = f32[512,4096]{1,0:T(8,128)} fusion(f32[512,4096]{1,0:T(8,128)} %get-tuple-element.245, f32[512]{0:T(512)S(1)} %bitcast.31, s32[512]{0:T(512)S(1)} %bitcast.32, pred[]{:T(512)S(6)} %compare.7), kind=kLoop, calls=%fused_computation.16.clone.1 | loop fusion | flops 8388608 | bytes 16781312 | tf_op jit(solution)/shard_map/while/body/eval_jaxpr/add | solution.py:26
  201.2 6.5 %select_add_fusion.2 = f32[512,4096]{1,0:T(8,128)} fusion(f32[512,4096]{1,0:T(8,128)} %get-tuple-element.245, f32[512]{0:T(512)S(1)} %bitcast.31, s32[512]{0:T(512)S(1)} %bitcast.32, pred[]{:T(512)S(6)} %compare.7), kind=kLoop, calls=%fused_computation.16.clone.1 | loop fusion | flops 8388608 | bytes 16781312 | tf_op jit(solution)/shard_map/while/body/eval_jaxpr/add | solution.py:26
  207.7 6.0 %fusion.11 = f32[4096,128]{1,0:T(8,128)} fusion(bf16[512,128]{1,0:T(8,128)(2,1)S(1)} %copy-done.1, f32[512,4096]{1,0:T(8,128)} %get-tuple-element.124), kind=kOutput, calls=%fused_computation.20 | convolution fusion | flops 538968064 | bytes 10616832 | tf_op jit(solution)/shard_map/dot_general | solution.py:53
  213.9 4.9 %fusion.15 = bf16[512,128]{0,1:T(8,128)(2,1)S(1)} fusion(bf16[4096,128]{1,0:T(8,128)(2,1)S(1)} %copy-done, f32[512,4096]{1,0:T(8,128)} %get-tuple-element.124), kind=kOutput, calls=%fused_computation.24 | convolution fusion | flops 539033600 | bytes 9568256 | tf_op jit(solution)/shard_map/dot_general | solution.py:49
  218.8 58.8 %reduce-scatter.2.cloned.1.call-done = f32[256,128]{1,0:T(8,128)} async-done(((f32[4096,128]{1,0:T(8,128)}), f32[256,128]{1,0:T(8,128)}) %reduce-scatter.2.cloned.1.call-update) | async-done | bytes 131088 | tf_op jit(solution)/shard_map/reduce_scatter | solution.py:56
  277.6 56.7 %while.25 = (s32[]{:T(128)}, f32[512,128]{1,0:T(8,128)S(1)}, s32[16,2048]{1,0:T(8,128)}, s32[16,2048]{1,0:T(8,128)}, bf16[16,2048,128]{2,1,0:T(8,128)(2,1)}, /*index=5*/s32[]{:T(128)}, s32[]{:T(128)}) while((s32[]{:T(128)}, f32[512,128]{1,0:T(8,128)S(1)}, s32[16,2048]{1,0:T(8,128)}, s32[16,2048]{1,0:T(8,128)}, ...), condition=%wide.region_1.2_spmd.clone, body=%wide.region_0.1_spmd.clone.sunk | while | flops 270667776 | bytes 1098335 | solution.py:44
  290.0 1.8 fusion.23
  297.1 1.8 fusion.23
  300.6 1.8 fusion.23
  304.2 1.8 fusion.23
  325.4 1.8 fusion.23
  335.3 2.4 reduce_sum.9
  (79 shorter events, 56.9 us)
Async XLA Ops:
  7.2 206.7 %copy-start = (bf16[4096,128]{1,0:T(8,128)(2,1)S(1)}, bf16[4096,128]{1,0:T(8,128)(2,1)}, u32[]{:S(2)}) copy-start(bf16[4096,128]{1,0:T(8,128)(2,1)} %param.16) | copy-start | bytes 3145732
  8.9 14.1 %all-to-all-start = ((s32[16,1,2048]{2,1,0:T(1,128)}), s32[16,1,2048]{2,1,0:T(1,128)S(1)}, u32[]{:S(2)}, u32[]{:S(2)}) async-start(s32[16,1,2048]{2,1,0:T(1,128)} %all_to_all.13), calls=%async_computation | async-start | bytes 262144 | tf_op jit(solution)/shard_map/all_to_all | solution.py:37
  145.8 131.9 %all-to-all-start.1 = ((bf16[16,2048,128]{2,1,0:T(8,128)(2,1)}), bf16[16,2048,128]{2,1,0:T(8,128)(2,1)}, u32[]{:S(2)}, u32[]{:S(2)}) async-start(bf16[16,2048,128]{2,1,0:T(8,128)(2,1)} %broadcast_select_fusion), calls=%async_computation.1 | async-start | bytes 16777216 | tf_op jit(solution)/shard_map/all_to_all | solution.py:39
  151.7 125.9 %reduce-scatter.2.cloned.1.call-start = ((), (), s32[]{:S(2)}) async-start(), calls=%async_computation.3 | async-start | bytes 2228224 | tf_op jit(solution)/shard_map/reduce_scatter | solution.py:56
  151.8 56.0 %copy-start.1 = (bf16[512,128]{1,0:T(8,128)(2,1)S(1)}, bf16[512,128]{1,0:T(8,128)(2,1)}, u32[]{:S(2)}) copy-start(bf16[512,128]{1,0:T(8,128)(2,1)} %param.19) | copy-start | bytes 393220
  213.8 121.5 %all-gather.3.cloned.1.call-start = ((), (), s32[]{:S(2)}) async-start(), calls=%async_computation.4 | async-start | bytes 2228224 | tf_op jit(solution)/shard_map/all_gather | solution.py:57
Sparse Core Ops, SparseCore 0:
  213.9 63.6 reduce-scatter.1
  280.0 48.7 all-gather.2
